TPU v7x, 512 devices: a whole 4x4x16 slice. The times are simulated.
512 devices in a mesh: src: 4 (over y), seq: 8 (over z_hi, core), head: 16 (over z_lo, x).
Axes of the slice: x: 4, y: 4, z: 16 (z_hi: 4, z_lo: 4; z = z_hi * 4 + z_lo), core: 2. Of those that a mesh axis runs over, the one named last changes fastest.
Arguments:
- enc_out: bfloat16 [32768, 4096], P(('src', 'seq'), 'head'), parts along dimension 0, may hold values from -9 to 9
- enc_gain: float32 [4096], replicated, may hold values from 0.25 to 1.75
- key_weight: bfloat16 [4096, 4096], P('seq', 'head'), may hold values from -1 to 1
- value_weight: bfloat16 [4096, 4096], P('seq', 'head'), may hold values from -0.09375 to 0.09375
- query_weight: bfloat16 [4096, 4096], P('seq', 'head'), may hold values from -2 to 2
- out_weight: bfloat16 [4096, 4096], P('head', 'seq'), may hold values from -0.09375 to 0.09375
- dec_gain: float32 [4096], replicated, may hold values from 0.25 to 1.75
- beam_state: float32 [64, 4096], P('src'), parts along dimension 0, may hold values from -7 to 7
- parents: int32 [8, 16], P('src'), parts along dimension 0, may hold values from 0 to 15
- token_embed: bfloat16 [8, 16, 4096], P('src'), parts along dimension 0, may hold values from -6 to 6
Outputs:
- final_state: float32 [64, 4096], P('src'), parts along dimension 0
- attended: float32 [64, 4096], P('src'), parts along dimension 0
There are 4 independent parts, one for each index of `src`. A program takes and returns all parts, laid end to end along the dimension named above; an argument that names none is the same for every part. Nothing has to cross between parts.
All inputs are finite; a program needn't handle non-finite values.
Results may differ from a plain program's by a relative error of at most 0.013.
The roundings to bfloat16 on the way count: a program that leaves them out, or rounds other values in their place, can miss the bound.
Values may be sent and summed in bfloat16 or wider, within the bound.
A program may use at most 64 MiB of HBM per device.

v0:
```python
import jax
import jax.numpy as jnp
from jax import lax
from jax.sharding import PartitionSpec as P

HEAD_DIM = 64
BEAMS = 16
STEPS = 2


def rms_norm(values, gain):
    mean_square = jnp.mean(values * values, axis=-1, keepdims=True)
    return values * lax.rsqrt(mean_square + 1e-06) * gain


def on_device(
    enc_out,
    enc_gain,
    key_weight,
    value_weight,
    query_weight,
    out_weight,
    dec_gain,
    beam_state,
    parents,
    token_embed,
):
    full_rows = lax.all_gather(enc_out, "head", axis=1, tiled=True)
    memory = rms_norm(full_rows.astype(jnp.float32), enc_gain).astype(jnp.bfloat16)
    key_full, value_full = (
        lax.all_gather(key_weight, "seq", axis=0, tiled=True),
        lax.all_gather(value_weight, "seq", axis=0, tiled=True),
    )
    rows = memory.shape[0]
    heads_here = key_weight.shape[1] // HEAD_DIM
    keys = jnp.dot(memory, key_full, preferred_element_type=jnp.float32).astype(jnp.bfloat16)
    values = jnp.dot(memory, value_full, preferred_element_type=jnp.float32).astype(jnp.bfloat16)
    keys = keys.reshape(rows, heads_here, HEAD_DIM)
    values = values.reshape(rows, heads_here, HEAD_DIM)
    feat_rows = query_weight.shape[0]
    feat_start = lax.axis_index("seq") * feat_rows
    state = beam_state
    attended = jnp.zeros(beam_state.shape, jnp.float32)
    for step in range(STEPS):
        state = jnp.take(state, parents[step], axis=0) + token_embed[step].astype(jnp.float32)
        normed = rms_norm(state, dec_gain).astype(jnp.bfloat16)
        normed_part = lax.dynamic_slice_in_dim(normed, feat_start, feat_rows, 1)
        query_part = jnp.dot(normed_part, query_weight, preferred_element_type=jnp.float32)
        query = lax.psum(query_part, "seq").astype(jnp.bfloat16)
        query = query.reshape(BEAMS, heads_here, HEAD_DIM)
        scores = jnp.einsum("bhd,shd->bhs", query, keys, preferred_element_type=jnp.float32) * 0.125
        top = jnp.max(scores, axis=-1)
        expo = jnp.exp(scores - top[..., None])
        total = jnp.sum(expo, axis=-1)
        weights = expo.astype(jnp.bfloat16)
        weighted = jnp.einsum("bhs,shd->bhd", weights, values, preferred_element_type=jnp.float32)
        peak_all = lax.pmax(top, "seq")
        factor = jnp.exp(top - peak_all)
        total_all, weighted_all = lax.psum((total * factor, weighted * factor[..., None]), "seq")
        context = (weighted_all / total_all[..., None]).astype(jnp.bfloat16)
        context = context.reshape(BEAMS, heads_here * HEAD_DIM)
        partial_out = jnp.dot(context, out_weight, preferred_element_type=jnp.float32)
        columns = lax.psum(partial_out.astype(jnp.bfloat16), "head").astype(jnp.float32)
        added = lax.all_gather(columns.astype(jnp.bfloat16), "seq", axis=1, tiled=True).astype(
            columns.dtype
        )
        state = state + added
        attended = attended + added
    return (state, attended)


def solution(mesh):
    placed = (
        P(("src", "seq"), "head"),
        P(),
        P("seq", "head"),
        P("seq", "head"),
        P("seq", "head"),
        P("head", "seq"),
        P(),
        P("src", None),
        P("src", None),
        P("src", None, None),
    )
    return jax.shard_map(
        on_device,
        mesh=mesh,
        in_specs=placed,
        out_specs=(P("src", None), P("src", None)),
        check_vma=False,
    )
```

profile of v0, /device:TPU:9, one launch (start us, length us, event | category | flops | bytes accessed | tf_op | source)
XLA Modules:
  0.0 602.1 jit_solution(18296726417365405977)
XLA Ops:
  7.2 0.0 copy-start
  7.2 0.0 copy-start.4
  7.2 0.0 all-gather.4.cloned.1.call-start
  7.2 0.7 all-gather.4.cloned.1.call-update
  7.9 0.0 all-gather.8.cloned.1.call-start
  8.0 0.7 all-gather.8.cloned.1.call-update
  8.7 0.0 all-gather.6.cloned.1.call-start
  8.7 0.7 all-gather.6.cloned.1.call-update
  9.4 0.8 compare_and_fusion
  10.2 0.0 copy-done
  10.2 0.6 gather_fusion
  10.8 0.8 dynamic-slice
  11.6 1.1 multiply_reduce_fusion.1
  12.7 1.1 fusion.29
  13.9 40.7 %psum.56 = bf16[16,256]{1,0:T(8,128)(2,1)S(1)} all-reduce(f32[16,256]{1,0:T(8,128)S(1)} %fusion.29), channel_id=1, replica_groups=mesh['src'=4,'seq'=8,'head'=16] {'seq'}, use_global_device_ids=true, to_apply=%region_2.4 | all-reduce | flops 4096 | bytes 24576 | tf_op jit(solution)/shard_map/psum | solution.py:49
  54.5 0.1 reshape.65
  54.6 78.1 %all-gather.4.cloned.1.call-done = bf16[1024,4096]{1,0:T(8,128)(2,1)} async-done(((bf16[1024,256]{1,0:T(8,128)(2,1)}), bf16[1024,4096]{1,0:T(8,128)(2,1)}) %all-gather.4.cloned.1.call-update) | async-done | bytes 8388624 | tf_op jit(solution)/shard_map/all_gather | solution.py:28
  132.8 5.1 fusion
  137.8 70.8 %all-gather.8.cloned.1.call-done = bf16[4096,256]{1,0:T(8,128)(2,1)} async-done(((bf16[512,256]{1,0:T(8,128)(2,1)}), bf16[4096,256]{1,0:T(8,128)(2,1)}) %all-gather.8.cloned.1.call-update) | async-done | bytes 2097168 | tf_op jit(solution)/shard_map/all_gather | solution.py:31
  208.6 0.0 copy-done.4
  208.6 6.6 %fusion.10 = bf16[1024,256]{0,1:T(8,128)(2,1)S(1)} fusion(bf16[4096,256]{1,0:T(8,128)(2,1)} %all-gather.8.cloned.1.call-done, bf16[1024,4096]{1,0:T(8,128)(2,1)} %all-gather.4.cloned.1.call-done, f32[4096]{0:T(1024)S(1)} %copy-done.4, f32[1024]{0:T(1024)S(1)} %add_rsqrt_fusion), kind=kOutput, calls=%fused_computation.10 | convolution fusion | flops 2164523008 | bytes 11030528 | tf_op jit(solution)/shard_map/dot_general | solution.py:36
  215.3 0.3 fusion.43
  215.5 21.9 %pmax.14 = f32[16,4]{0,1:T(4,128)S(1)} all-reduce(f32[16,4]{0,1:T(4,128)S(1)} %get-tuple-element.23), channel_id=1, replica_groups=mesh['src'=4,'seq'=8,'head'=16] {'seq'}, use_global_device_ids=true, to_apply=%region_4.6 | all-reduce | flops 64 | bytes 512 | tf_op jit(solution)/shard_map/pmax | solution.py:57
  237.4 0.2 fusion.17
  237.6 0.0 copy-start.2
  237.6 0.0 copy-start.3
  237.6 0.0 copy-start.1
  237.6 28.6 %all-gather.6.cloned.1.call-done = bf16[4096,256]{1,0:T(8,128)(2,1)} async-done(((bf16[512,256]{1,0:T(8,128)(2,1)}), bf16[4096,256]{1,0:T(8,128)(2,1)}) %all-gather.6.cloned.1.call-update) | async-done | bytes 2097168 | tf_op jit(solution)/shard_map/all_gather | solution.py:32
  266.2 6.6 %fusion.7 = bf16[1024,256]{0,1:T(8,128)(2,1)S(1)} fusion(bf16[4096,256]{1,0:T(8,128)(2,1)} %all-gather.6.cloned.1.call-done, bf16[1024,4096]{1,0:T(8,128)(2,1)} %all-gather.4.cloned.1.call-done, f32[4096]{0:T(1024)S(1)} %copy-done.4, f32[1024]{0:T(1024)S(1)} %add_rsqrt_fusion), kind=kOutput, calls=%fused_computation.9 | convolution fusion | flops 2164523008 | bytes 11030528 | tf_op jit(solution)/shard_map/dot_general | solution.py:37
  272.8 0.3 fusion.16
  273.1 34.6 %all-reduce.1 = (f32[16,4,64]{2,0,1:T(8,128)S(1)}, f32[16,4]{0,1:T(4,128)S(1)}) all-reduce(f32[16,4,64]{2,0,1:T(8,128)S(1)} %fusion.16, f32[16,4]{0,1:T(4,128)S(1)} %get-tuple-element.13), channel_id=1, replica_groups=mesh['src'=4,'seq'=8,'head'=16] {'seq'}, use_global_device_ids=true, to_apply=%region_5.7 | all-reduce | flops 4160 | bytes 33280 | tf_op jit(solution)/shard_map/psum | solution.py:59
  307.7 0.1 divide_convert_fusion.1
  307.8 0.1 reshape.66
  307.9 0.0 copy-done.2
  307.9 0.1 convolution_convert_fusion.1
  308.0 64.0 %psum.59 = bf16[16,512]{1,0:T(8,128)(2,1)S(1)} all-reduce(bf16[16,512]{1,0:T(8,128)(2,1)S(1)} %convolution_convert_fusion.1), channel_id=1, replica_groups=mesh['src'=4,'seq'=8,'head'=16] {'head'}, use_global_device_ids=true, to_apply=%region_8.10 | all-reduce | flops 8192 | bytes 32768 | tf_op jit(solution)/shard_map/psum | solution.py:63
  372.1 35.7 %all_gather.18 = bf16[16,4096]{1,0:T(8,128)(2,1)S(1)} all-gather(bf16[16,512]{1,0:T(8,128)(2,1)S(1)} %psum.59), channel_id=1, replica_groups=mesh['src'=4,'seq'=8,'head'=16] {'seq'}, dimensions={1}, use_global_device_ids=true | all-gather | bytes 147456 | tf_op jit(solution)/shard_map/all_gather | solution.py:64
  407.8 0.6 gather_fusion.1
  408.5 0.0 copy-done.3
  408.5 0.2 multiply_reduce_fusion
  408.7 0.0 copy-done.1
  408.7 0.2 fusion.31
  408.9 33.7 %psum.60 = bf16[16,256]{1,0:T(8,128)(2,1)S(1)} all-reduce(f32[16,256]{1,0:T(8,128)S(1)} %fusion.31), channel_id=1, replica_groups=mesh['src'=4,'seq'=8,'head'=16] {'seq'}, use_global_device_ids=true, to_apply=%region_10.12 | all-reduce | flops 4096 | bytes 24576 | tf_op jit(solution)/shard_map/psum | solution.py:49
  442.6 0.1 reshape.67
  442.7 0.3 fusion.44
  443.0 20.1 %pmax.15 = f32[16,4]{0,1:T(4,128)S(1)} all-reduce(f32[16,4]{0,1:T(4,128)S(1)} %get-tuple-element.25), channel_id=1, replica_groups=mesh['src'=4,'seq'=8,'head'=16] {'seq'}, use_global_device_ids=true, to_apply=%region_12.14 | all-reduce | flops 64 | bytes 512 | tf_op jit(solution)/shard_map/pmax | solution.py:57
  463.1 0.2 fusion.19
  463.3 0.3 fusion.15
  463.6 35.0 %all-reduce = (f32[16,4,64]{2,0,1:T(8,128)S(1)}, f32[16,4]{0,1:T(4,128)S(1)}) all-reduce(f32[16,4,64]{2,0,1:T(8,128)S(1)} %fusion.15, f32[16,4]{0,1:T(4,128)S(1)} %get-tuple-element.7), channel_id=1, replica_groups=mesh['src'=4,'seq'=8,'head'=16] {'seq'}, use_global_device_ids=true, to_apply=%region_13.15 | all-reduce | flops 4160 | bytes 33280 | tf_op jit(solution)/shard_map/psum | solution.py:59
  498.5 0.1 divide_convert_fusion
  498.6 0.1 reshape.68
  498.7 0.1 convolution_convert_fusion
  498.9 60.6 %psum.63 = bf16[16,512]{1,0:T(8,128)(2,1)S(1)} all-reduce(bf16[16,512]{1,0:T(8,128)(2,1)S(1)} %convolution_convert_fusion), channel_id=1, replica_groups=mesh['src'=4,'seq'=8,'head'=16] {'head'}, use_global_device_ids=true, to_apply=%region_16.18 | all-reduce | flops 8192 | bytes 32768 | tf_op jit(solution)/shard_map/psum | solution.py:63
  559.5 35.3 %all_gather.19 = bf16[16,4096]{1,0:T(8,128)(2,1)S(1)} all-gather(bf16[16,512]{1,0:T(8,128)(2,1)S(1)} %psum.63), channel_id=1, replica_groups=mesh['src'=4,'seq'=8,'head'=16] {'seq'}, dimensions={1}, use_global_device_ids=true | all-gather | bytes 147456 | tf_op jit(solution)/shard_map/all_gather | solution.py:64
  594.8 0.8 convert_add_fusion
  (10 shorter events, 0.1 us)
Async XLA Ops:
  7.2 3.0 copy-start
  7.2 201.4 %copy-start.4 = (f32[4096]{0:T(1024)S(1)}, f32[4096]{0:T(1024)}, u32[]{:S(2)}) copy-start(f32[4096]{0:T(1024)} %param.13) | copy-start | bytes 49156
  7.2 125.6 %all-gather.4.cloned.1.call-start = ((), (), s32[]{:S(2)}) async-start(), calls=%async_computation | async-start | bytes 8912896 | tf_op jit(solution)/shard_map/all_gather | solution.py:28
  7.9 200.7 %all-gather.8.cloned.1.call-start = ((), (), s32[]{:S(2)}) async-start(), calls=%async_computation.2 | async-start | bytes 2359296 | tf_op jit(solution)/shard_map/all_gather | solution.py:31
  8.7 257.5 %all-gather.6.cloned.1.call-start = ((), (), s32[]{:S(2)}) async-start(), calls=%async_computation.1 | async-start | bytes 2359296 | tf_op jit(solution)/shard_map/all_gather | solution.py:32
  237.6 70.3 %copy-start.2 = (bf16[256,512]{1,0:T(8,128)(2,1)S(1)}, bf16[256,512]{1,0:T(8,128)(2,1)}, u32[]{:S(2)}) copy-start(bf16[256,512]{1,0:T(8,128)(2,1)} %param.17) | copy-start | bytes 786436
  237.6 170.9 %copy-start.3 = (bf16[2,16,4096]{2,1,0:T(8,128)(2,1)S(1)}, bf16[2,16,4096]{2,1,0:T(8,128)(2,1)}, u32[]{:S(2)}) copy-start(bf16[2,16,4096]{2,1,0:T(8,128)(2,1)} %param.21) | copy-start | bytes 786436
  237.6 171.1 %copy-start.1 = (bf16[512,256]{1,0:T(8,128)(2,1)S(1)}, bf16[512,256]{1,0:T(8,128)(2,1)}, u32[]{:S(2)}) copy-start(bf16[512,256]{1,0:T(8,128)(2,1)} %param.16) | copy-start | bytes 786436
Sparse Core Ops, SparseCore 0:
  10.0 122.7 all-gather.3
  134.9 73.6 all-gather.7
  210.8 55.3 all-gather.5
where the time goes:
time: 603 us; the launch traced here: 602 us
  blocking collectives  382 us (63%)
  waiting for transfers between devices  180 us (30%)
  matrix products  15.9 us (3%)
  between operations  13.9 us (2%)
  other arithmetic  8.64 us (1%)
    psum x2, blocking collectives, on_device(): lax.psum(partial_out.astype(jnp.bfloat16), 'head').astype(jnp.float32)  125 us
    all_gather x1, waiting for transfers between devices, on_device(): full_rows = lax.all_gather(enc_out, 'head', axis=1, tiled=True)  78.1 us
    psum x2, blocking collectives, on_device(): query = lax.psum(query_part, 'seq').astype(jnp.bfloat16)  74.3 us
    all_gather x2, blocking collectives, on_device(): lax.all_gather(columns.astype(jnp.bfloat16), 'seq', axis=1, tiled=True)  71 us
    all_gather x1, waiting for transfers between devices, on_device(): lax.all_gather(key_weight, 'seq', axis=0, tiled=True)  70.8 us
    psum x2, blocking collectives, on_device(): lax.psum((total * factor, weighted * factor[..., None]), 'seq')  69.6 us
    pmax x2, blocking collectives, on_device(): peak_all = lax.pmax(top, 'seq')  42 us
    all_gather x1, waiting for transfers between devices, on_device(): lax.all_gather(value_weight, 'seq', axis=0, tiled=True)  28.6 us
  transfers between devices with their start and end apart: 3, of which 3 were waited for; matrix products, arithmetic and copies ran while one was open for 3% of the time, Pallas kernels for 0%

commit v1 on v0

--- a/solution.py
+++ b/solution.py
@@ -28,7 +28,9 @@
     full_rows = lax.all_gather(enc_out, "head", axis=1, tiled=True)
     memory = rms_norm(full_rows.astype(jnp.float32), enc_gain).astype(jnp.bfloat16)
     key_full, value_full = (
-        lax.all_gather(key_weight, "seq", axis=0, tiled=True),
+        jnp.concatenate(
+            lax.all_to_all(jnp.stack([key_weight] * lax.axis_size("seq")), "seq", 0, 0), axis=0
+        ),
         lax.all_gather(value_weight, "seq", axis=0, tiled=True),
     )
     rows = memory.shape[0]

time: 603 us -> 626 us (1.038)
  blocking collectives: 382 us -> 472 us
  waiting for transfers between devices: 180 us -> 96.4 us
  starting transfers between devices: 0.11 us -> 15.9 us
    psum x2, blocking collectives: 74.3 us -> 156 us  [on_device(): query = lax.psum(query_part, 'seq').astype(jnp.bfloat16)]
    all_gather x1 -> x0, waiting for transfers between devices: 70.8 us -> none  [on_device(): lax.all_gather(key_weight, 'seq', axis=0, tiled=True)]
    all_to_all x0 -> x1, starting transfers between devices: none -> 15.9 us  [on_device(): lax.all_to_all(jnp.stack([key_weight] * lax.axis_size('seq')), 'seq', 0, 0)]
    all_gather x1, waiting for transfers between devices: 78.1 us -> 66.7 us  [on_device(): full_rows = lax.all_gather(enc_out, 'head', axis=1, tiled=True)]
    pmax x2, blocking collectives: 42 us -> 50.1 us  [on_device(): peak_all = lax.pmax(top, 'seq')]
  transfers between devices with their start and end apart: 3 -> 3, of which waited for: 3 -> 2; matrix products, arithmetic and copies ran while one was open for 3% -> 3% of each run, Pallas kernels for 0% -> 0%
where the time goes in v1:
time: 626 us
  blocking collectives  472 us (75%)
  waiting for transfers between devices  96.4 us (15%)
  starting transfers between devices  15.9 us (3%)
  matrix products  14.6 us (2%)
  between operations  14.2 us (2%)
  other arithmetic  7.75 us (1%)
    psum x2, blocking collectives, on_device(): query = lax.psum(query_part, 'seq').astype(jnp.bfloat16)  156 us
    psum x2, blocking collectives, on_device(): lax.psum(partial_out.astype(jnp.bfloat16), 'head').astype(jnp.float32)  124 us
    all_gather x2, blocking collectives, on_device(): lax.all_gather(columns.astype(jnp.bfloat16), 'seq', axis=1, tiled=True)  71.6 us
    psum x2, blocking collectives, on_device(): lax.psum((total * factor, weighted * factor[..., None]), 'seq')  69.6 us
    all_gather x1, waiting for transfers between devices, on_device(): full_rows = lax.all_gather(enc_out, 'head', axis=1, tiled=True)  66.7 us
    pmax x2, blocking collectives, on_device(): peak_all = lax.pmax(top, 'seq')  50.1 us
    all_gather x1, waiting for transfers between devices, on_device(): lax.all_gather(value_weight, 'seq', axis=0, tiled=True)  28.3 us
    all_to_all x1, starting transfers between devices, on_device(): lax.all_to_all(jnp.stack([key_weight] * lax.axis_size('seq')), 'seq', 0, 0)  15.9 us
  transfers between devices with their start and end apart: 3, of which 2 were waited for; matrix products, arithmetic and copies ran while one was open for 3% of the time, Pallas kernels for 0%

profile of v1, /device:TPU:9, one launch (start us, length us, event | category | flops | bytes accessed | tf_op | source)
XLA Modules:
  0.0 625.6 jit_solution(8986663522904140282)
XLA Ops:
  7.2 0.0 copy-start
  7.2 0.0 copy-start.3
  7.2 0.0 copy-start.1
  7.2 0.0 all-gather.3.cloned.1.call-start
  7.2 0.7 all-gather.3.cloned.1.call-update
  7.9 2.4 stack.2
  10.3 0.0 copy-start.5
  10.3 15.9 %all-to-all-start = ((bf16[8,512,256]{2,1,0:T(8,128)(2,1)}), bf16[8,512,256]{2,1,0:T(8,128)(2,1)S(1)}, u32[]{:S(2)}, u32[]{:S(2)}) async-start(bf16[8,512,256]{2,1,0:T(8,128)(2,1)} %stack.2), calls=%async_computation | async-start | bytes 4194304 | tf_op jit(solution)/shard_map/all_to_all | solution.py:32
  26.2 0.0 all-gather.5.cloned.1.call-start
  26.2 0.7 all-gather.5.cloned.1.call-update
  27.0 0.8 dynamic-slice
  27.7 0.8 compare_and_fusion
  28.5 0.0 copy-done
  28.5 0.6 gather_fusion
  29.1 0.0 copy-done.3
  29.2 0.2 multiply_reduce_fusion.1
  29.4 0.0 copy-done.1
  29.4 0.2 fusion.29
  29.6 122.8 %psum.56 = bf16[16,256]{1,0:T(8,128)(2,1)S(1)} all-reduce(f32[16,256]{1,0:T(8,128)S(1)} %fusion.29), channel_id=1, replica_groups=mesh['src'=4,'seq'=8,'head'=16] {'seq'}, use_global_device_ids=true, to_apply=%region_2.4 | all-reduce | flops 4096 | bytes 24576 | tf_op jit(solution)/shard_map/psum | solution.py:51
  152.4 0.1 reshape.71
  152.5 66.7 %all-gather.3.cloned.1.call-done = bf16[1024,4096]{1,0:T(8,128)(2,1)} async-done(((bf16[1024,256]{1,0:T(8,128)(2,1)}), bf16[1024,4096]{1,0:T(8,128)(2,1)}) %all-gather.3.cloned.1.call-update) | async-done | bytes 8388624 | tf_op jit(solution)/shard_map/all_gather | solution.py:28
  219.2 5.1 fusion
  224.3 0.0 all-to-all-done
  224.3 0.0 copy-done.5
  224.3 6.2 fusion.10
  230.5 0.3 fusion.43
  230.8 30.1 %pmax.14 = f32[16,4]{0,1:T(4,128)S(1)} all-reduce(f32[16,4]{0,1:T(4,128)S(1)} %get-tuple-element.23), channel_id=1, replica_groups=mesh['src'=4,'seq'=8,'head'=16] {'seq'}, use_global_device_ids=true, to_apply=%region_4.6 | all-reduce | flops 64 | bytes 512 | tf_op jit(solution)/shard_map/pmax | solution.py:59
  260.8 0.2 fusion.17
  261.0 0.0 copy-start.2
  261.1 0.0 copy-start.4
  261.1 28.3 %all-gather.5.cloned.1.call-done = bf16[4096,256]{1,0:T(8,128)(2,1)} async-done(((bf16[512,256]{1,0:T(8,128)(2,1)}), bf16[4096,256]{1,0:T(8,128)(2,1)}) %all-gather.5.cloned.1.call-update) | async-done | bytes 2097168 | tf_op jit(solution)/shard_map/all_gather | solution.py:34
  289.4 6.6 %fusion.7 = bf16[1024,256]{0,1:T(8,128)(2,1)S(1)} fusion(bf16[4096,256]{1,0:T(8,128)(2,1)} %all-gather.5.cloned.1.call-done, bf16[1024,4096]{1,0:T(8,128)(2,1)} %all-gather.3.cloned.1.call-done, f32[4096]{0:T(1024)S(1)} %copy-done.5, f32[1024]{0:T(1024)S(1)} %add_rsqrt_fusion), kind=kOutput, calls=%fused_computation.9 | convolution fusion | flops 2164523008 | bytes 11030528 | tf_op jit(solution)/shard_map/dot_general | solution.py:39
  296.0 0.3 fusion.16
  296.3 34.6 %all-reduce.1 = (f32[16,4,64]{2,0,1:T(8,128)S(1)}, f32[16,4]{0,1:T(4,128)S(1)}) all-reduce(f32[16,4,64]{2,0,1:T(8,128)S(1)} %fusion.16, f32[16,4]{0,1:T(4,128)S(1)} %get-tuple-element.13), channel_id=1, replica_groups=mesh['src'=4,'seq'=8,'head'=16] {'seq'}, use_global_device_ids=true, to_apply=%region_5.7 | all-reduce | flops 4160 | bytes 33280 | tf_op jit(solution)/shard_map/psum | solution.py:61
  330.9 0.1 divide_convert_fusion.1
  331.0 0.1 reshape.72
  331.1 0.0 copy-done.2
  331.1 0.1 convolution_convert_fusion.1
  331.3 63.8 %psum.59 = bf16[16,512]{1,0:T(8,128)(2,1)S(1)} all-reduce(bf16[16,512]{1,0:T(8,128)(2,1)S(1)} %convolution_convert_fusion.1), channel_id=1, replica_groups=mesh['src'=4,'seq'=8,'head'=16] {'head'}, use_global_device_ids=true, to_apply=%region_8.10 | all-reduce | flops 8192 | bytes 32768 | tf_op jit(solution)/shard_map/psum | solution.py:65
  395.0 35.9 %all_gather.14 = bf16[16,4096]{1,0:T(8,128)(2,1)S(1)} all-gather(bf16[16,512]{1,0:T(8,128)(2,1)S(1)} %psum.59), channel_id=1, replica_groups=mesh['src'=4,'seq'=8,'head'=16] {'seq'}, dimensions={1}, use_global_device_ids=true | all-gather | bytes 147456 | tf_op jit(solution)/shard_map/all_gather | solution.py:66
  431.0 0.6 gather_fusion.1
  431.6 0.0 copy-done.4
  431.7 0.2 multiply_reduce_fusion
  431.9 0.2 fusion.31
  432.1 33.7 %psum.60 = bf16[16,256]{1,0:T(8,128)(2,1)S(1)} all-reduce(f32[16,256]{1,0:T(8,128)S(1)} %fusion.31), channel_id=1, replica_groups=mesh['src'=4,'seq'=8,'head'=16] {'seq'}, use_global_device_ids=true, to_apply=%region_10.12 | all-reduce | flops 4096 | bytes 24576 | tf_op jit(solution)/shard_map/psum | solution.py:51
  465.8 0.1 reshape.73
  465.8 0.3 fusion.44
  466.1 20.0 %pmax.15 = f32[16,4]{0,1:T(4,128)S(1)} all-reduce(f32[16,4]{0,1:T(4,128)S(1)} %get-tuple-element.25), channel_id=1, replica_groups=mesh['src'=4,'seq'=8,'head'=16] {'seq'}, use_global_device_ids=true, to_apply=%region_12.14 | all-reduce | flops 64 | bytes 512 | tf_op jit(solution)/shard_map/pmax | solution.py:59
  486.1 0.2 fusion.19
  486.3 0.3 fusion.15
  486.6 35.0 %all-reduce = (f32[16,4,64]{2,0,1:T(8,128)S(1)}, f32[16,4]{0,1:T(4,128)S(1)}) all-reduce(f32[16,4,64]{2,0,1:T(8,128)S(1)} %fusion.15, f32[16,4]{0,1:T(4,128)S(1)} %get-tuple-element.7), channel_id=1, replica_groups=mesh['src'=4,'seq'=8,'head'=16] {'seq'}, use_global_device_ids=true, to_apply=%region_13.15 | all-reduce | flops 4160 | bytes 33280 | tf_op jit(solution)/shard_map/psum | solution.py:61
  521.5 0.1 divide_convert_fusion
  521.6 0.1 reshape.74
  521.7 0.1 convolution_convert_fusion
  521.9 60.4 %psum.63 = bf16[16,512]{1,0:T(8,128)(2,1)S(1)} all-reduce(bf16[16,512]{1,0:T(8,128)(2,1)S(1)} %convolution_convert_fusion), channel_id=1, replica_groups=mesh['src'=4,'seq'=8,'head'=16] {'head'}, use_global_device_ids=true, to_apply=%region_16.18 | all-reduce | flops 8192 | bytes 32768 | tf_op jit(solution)/shard_map/psum | solution.py:65
  582.2 35.7 %all_gather.15 = bf16[16,4096]{1,0:T(8,128)(2,1)S(1)} all-gather(bf16[16,512]{1,0:T(8,128)(2,1)S(1)} %psum.63), channel_id=1, replica_groups=mesh['src'=4,'seq'=8,'head'=16] {'seq'}, dimensions={1}, use_global_device_ids=true | all-gather | bytes 147456 | tf_op jit(solution)/shard_map/all_gather | solution.py:66
  617.9 0.8 convert_add_fusion
  (10 shorter events, 0.1 us)
Async XLA Ops:
  7.2 21.3 %copy-start = (f32[16,4096]{1,0:T(8,128)S(1)}, f32[16,4096]{1,0:T(8,128)}, u32[]{:S(2)}) copy-start(f32[16,4096]{1,0:T(8,128)} %param.19) | copy-start | bytes 786436
  7.2 22.0 %copy-start.3 = (bf16[2,16,4096]{2,1,0:T(8,128)(2,1)S(1)}, bf16[2,16,4096]{2,1,0:T(8,128)(2,1)}, u32[]{:S(2)}) copy-start(bf16[2,16,4096]{2,1,0:T(8,128)(2,1)} %param.21) | copy-start | bytes 786436
  7.2 22.2 %copy-start.1 = (bf16[512,256]{1,0:T(8,128)(2,1)S(1)}, bf16[512,256]{1,0:T(8,128)(2,1)}, u32[]{:S(2)}) copy-start(bf16[512,256]{1,0:T(8,128)(2,1)} %param.16) | copy-start | bytes 786436
  7.2 212.0 %all-gather.3.cloned.1.call-start = ((), (), s32[]{:S(2)}) async-start(), calls=%async_computation.1 | async-start | bytes 8912896 | tf_op jit(solution)/shard_map/all_gather | solution.py:28
  10.3 214.0 %copy-start.5 = (f32[4096]{0:T(1024)S(1)}, f32[4096]{0:T(1024)}, u32[]{:S(2)}) copy-start(f32[4096]{0:T(1024)} %param.13) | copy-start | bytes 49156
  10.3 213.9 %all-to-all-start = ((bf16[8,512,256]{2,1,0:T(8,128)(2,1)}), bf16[8,512,256]{2,1,0:T(8,128)(2,1)S(1)}, u32[]{:S(2)}, u32[]{:S(2)}) async-start(bf16[8,512,256]{2,1,0:T(8,128)(2,1)} %stack.2), calls=%async_computation | async-start | bytes 4194304 | tf_op jit(solution)/shard_map/all_to_all | solution.py:32
  26.2 263.2 %all-gather.5.cloned.1.call-start = ((), (), s32[]{:S(2)}) async-start(), calls=%async_computation.2 | async-start | bytes 2359296 | tf_op jit(solution)/shard_map/all_gather | solution.py:34
  261.0 70.1 %copy-start.2 = (bf16[256,512]{1,0:T(8,128)(2,1)S(1)}, bf16[256,512]{1,0:T(8,128)(2,1)}, u32[]{:S(2)}) copy-start(bf16[256,512]{1,0:T(8,128)(2,1)} %param.17) | copy-start | bytes 786436
  261.1 170.6 %copy-start.4 = (bf16[2,16,4096]{2,1,0:T(8,128)(2,1)S(1)}, bf16[2,16,4096]{2,1,0:T(8,128)(2,1)}, u32[]{:S(2)}) copy-start(bf16[2,16,4096]{2,1,0:T(8,128)(2,1)} %param.21) | copy-start | bytes 786436
Sparse Core Ops, SparseCore 0:
  10.0 209.1 all-gather.2
  221.3 68.0 all-gather.4
